TPU v7x, 32 devices: a whole 2x2x4 slice. The times are simulated.
32 devices in a mesh: wide: 8 (over y, x, core), narrow: 4 (over z).
Axes of the slice: x: 2, y: 2, z: 4, core: 2. Of those that a mesh axis runs over, the one named last changes fastest.
Arguments:
- activity: bfloat16 [32, 8, 512, 512], P(('wide', 'narrow')), may hold values from 0 to 1
- tile_coords: int32 [32, 2], replicated, may hold values from 0 to 7, as said below
- user_owner: int32 [8], replicated, may hold values from 0 to 7, each once
- item_owner: int32 [8], replicated, may hold values from 0 to 7, each once
- user_factor: float32 [4096, 256], P('wide', 'narrow'), may hold values from 0 to 1
- item_factor: float32 [4096, 256], P('wide', 'narrow'), may hold values from 0 to 1
- time_factor: float32 [8, 256], replicated, may hold values from 0.0003 to 0.003
- user_dual: float32 [4096, 256], P('wide', 'narrow'), may hold values from -1.8 to 1.8
- item_dual: float32 [4096, 256], P('wide', 'narrow'), may hold values from -1.8 to 1.8
Outputs:
- new_users: float32 [4096, 256], P('wide', 'narrow')
- new_items: float32 [4096, 256], P('wide', 'narrow')
- new_user_dual: float32 [4096, 256], P('wide', 'narrow')
- new_item_dual: float32 [4096, 256], P('wide', 'narrow')
Inputs may be any that keep to these rules, and one draw needn't show every extreme that they name: `tile_coords`: no pair of blocks appears twice. `user_owner`: each stored row block holds exactly one user block. `item_owner`: each stored row block holds exactly one item block.
All inputs are finite; a program needn't handle non-finite values.
Results may differ from a plain program's by a relative error of at most 0.0017.
The roundings to bfloat16 on the way count: a program that leaves them out, or rounds other values in their place, can miss the bound.
Values may be sent and summed in bfloat16 or wider, within the bound.
No kernel may reach another device: no remote copies, remote signals or barrier semaphores. Data moves between devices by JAX's collectives and lax.ppermute only.
A program may use at most 64 MiB of HBM per device.

v0:
```python
import jax
import jax.numpy as jnp
from jax import lax
from jax.sharding import PartitionSpec as P

RANK = 256
BLOCK = 512
PASSES = 2


def locate(owner, wanted_blocks):
    everyone = jnp.arange(owner.shape[0], dtype=jnp.int32)
    chosen = jnp.where(everyone[None, :] == wanted_blocks[:, None], owner[None, :], 0)
    return jnp.sum(chosen, axis=1)


def fetch_rows(factor, wanted):
    lowered = factor.astype(jnp.bfloat16)
    width = factor.shape[1]
    slots = wanted.shape[0]
    initial = jnp.zeros((slots, BLOCK, width), jnp.bfloat16)
    portion = lax.all_gather(lowered, "wide", axis=0, tiled=True)
    count_blocks = portion.shape[0] // BLOCK
    shaped = portion.reshape(count_blocks, BLOCK, width)
    first = jnp.int32(0) // BLOCK
    onehot = (wanted[:, None] == first + jnp.arange(count_blocks, dtype=jnp.int32)[None, :]).astype(
        jnp.bfloat16
    )
    picked = jnp.einsum("jq,qrc->jrc", onehot, shaped, preferred_element_type=jnp.float32)
    gathered = initial + picked.astype(jnp.bfloat16)
    return lax.all_to_all(gathered, "narrow", split_axis=0, concat_axis=2, tiled=True)


def tile_sums(activity, fetched, time_factor, forward):
    khatri = (fetched.astype(jnp.float32)[:, None] * time_factor[None, :, None, :]).astype(
        jnp.bfloat16
    )
    if forward:
        return jnp.einsum("tkij,tkjr->tir", activity, khatri, preferred_element_type=jnp.float32)
    return jnp.einsum("tkij,tkir->tjr", activity, khatri, preferred_element_type=jnp.float32)


def owner_sums(partial_value, targets, owned):
    received = lax.all_to_all(partial_value, "narrow", split_axis=2, concat_axis=0, tiled=True)
    width = received.shape[2]
    count_blocks = owned * lax.axis_size("wide") // BLOCK
    onehot = (jnp.arange(count_blocks, dtype=jnp.int32)[:, None] == targets[None, :]).astype(
        jnp.float32
    )
    placed = jnp.einsum("qj,jrc->qrc", onehot, received, precision=lax.Precision.HIGHEST)
    return lax.psum_scatter(
        placed.reshape(owned * lax.axis_size("wide"), width),
        "wide",
        scatter_dimension=0,
        tiled=True,
    )


def joint_gram(other_rows, time_factor):
    local_gram = jnp.dot(other_rows.T, other_rows, precision=lax.Precision.HIGHEST)
    total = lax.psum(local_gram, ("wide", "narrow"))
    gram = total * jnp.dot(time_factor.T, time_factor, precision=lax.Precision.HIGHEST)
    penalty = jnp.trace(gram) / RANK
    identity = jnp.eye(RANK, dtype=jnp.float32)
    lower = jnp.linalg.cholesky(gram + penalty * identity)
    inverse = jax.scipy.linalg.cho_solve((lower, True), identity)
    return (penalty, inverse)


def update_rows(
    activity, other_cols, other_rows, factor, dual, wanted, targets, time_factor, forward, owned
):
    fetched = fetch_rows(other_cols, wanted)
    partial_value = tile_sums(activity, fetched, time_factor, forward)
    sums = owner_sums(partial_value, targets, owned)
    sums_rows = lax.all_to_all(sums, "narrow", split_axis=0, concat_axis=1, tiled=True)
    penalty, inverse = joint_gram(other_rows, time_factor)
    for _ in range(PASSES):
        target = jnp.dot(
            sums_rows + penalty * (factor + dual), inverse, precision=lax.Precision.HIGHEST
        )
        factor = jnp.maximum(target - dual, 0.0)
        dual = dual + factor - target
    factor_cols, dual_cols = (
        lax.all_to_all(factor, "narrow", split_axis=1, concat_axis=0, tiled=True),
        lax.all_to_all(dual, "narrow", split_axis=1, concat_axis=0, tiled=True),
    )
    return (factor_cols, dual_cols, factor)


def local(
    activity,
    tile_coords,
    user_owner,
    item_owner,
    user_factor,
    item_factor,
    time_factor,
    user_dual,
    item_dual,
):
    narrow_size = lax.axis_size("narrow")
    slots = narrow_size * activity.shape[0]
    group_coords = lax.dynamic_slice_in_dim(tile_coords, lax.axis_index("wide") * slots, slots, 0)
    user_pos = locate(user_owner, group_coords[:, 0])
    item_pos = locate(item_owner, group_coords[:, 1])
    owned = user_factor.shape[0]
    user_rows, udual_rows, item_rows, idual_rows = (
        lax.all_to_all(user_factor, "narrow", split_axis=0, concat_axis=1, tiled=True),
        lax.all_to_all(user_dual, "narrow", split_axis=0, concat_axis=1, tiled=True),
        lax.all_to_all(item_factor, "narrow", split_axis=0, concat_axis=1, tiled=True),
        lax.all_to_all(item_dual, "narrow", split_axis=0, concat_axis=1, tiled=True),
    )
    new_users, new_user_dual, fresh_rows = update_rows(
        activity,
        item_factor,
        item_rows,
        user_rows,
        udual_rows,
        item_pos,
        user_pos,
        time_factor,
        True,
        owned,
    )
    new_items, new_item_dual, _ = update_rows(
        activity,
        new_users,
        fresh_rows,
        item_rows,
        idual_rows,
        user_pos,
        item_pos,
        time_factor,
        False,
        owned,
    )
    return (new_users, new_items, new_user_dual, new_item_dual)


def solution(mesh):
    in_specs = (
        P(("wide", "narrow"), None, None, None),
        P(),
        P(),
        P(),
        P("wide", "narrow"),
        P("wide", "narrow"),
        P(),
        P("wide", "narrow"),
        P("wide", "narrow"),
    )
    out_specs = (P("wide", "narrow"), P("wide", "narrow"), P("wide", "narrow"), P("wide", "narrow"))
    return jax.shard_map(local, mesh=mesh, in_specs=in_specs, out_specs=out_specs, check_vma=False)
```

profile of v0, /device:TPU:0, one launch (start us, length us, event | category | flops | bytes accessed | tf_op | source)
XLA Modules:
  0.0 562.6 jit_solution(15027327676209226072)
XLA Ops:
  9.6 6.3 %all-to-all-start.3 = ((f32[4,128,64]{1,2,0:T(8,128)}), f32[4,128,64]{1,2,0:T(8,128)S(1)}, u32[]{:S(2)}, u32[]{:S(2)}) async-start(f32[4,128,64]{1,2,0:T(8,128)} %copy_bitcast_fusion.8), calls=%async_computation.4 | async-start | bytes 262144 | tf_op jit(solution)/shard_map/all_to_all | solution.py:111
  16.9 9.9 %all_gather.6 = bf16[4096,64]{0,1:T(8,128)(2,1)S(1)} all-gather(bf16[512,64]{0,1:T(8,128)(2,1)S(1)} %convert_element_type.70), channel_id=1, replica_groups=mesh['wide'=8,'narrow'=4] {'wide'}, dimensions={0}, use_global_device_ids=true | all-gather | bytes 589824 | tf_op jit(solution)/shard_map/all_gather | solution.py:22
  33.5 5.1 all-to-all-start.4
  39.7 5.3 all-to-all-done.4
  49.3 5.1 all-to-all-done.5
  57.8 116.1 %all-reduce.4.cloned.1.call-done = f32[256,256]{0,1:T(8,128)} async-done(((f32[256,256]{0,1:T(8,128)}), f32[256,256]{0,1:T(8,128)}) %all-reduce.4.cloned.1.call-update) | async-done | bytes 262160 | tf_op jit(solution)/shard_map/psum | solution.py:61
  176.8 11.7 %cholesky.130 = f32[128,128]{1,0:T(8,128)S(1)} custom-call(f32[128,128]{1,0:T(8,128)S(1)} %cholesky.194), custom_call_target="Cholesky" | custom-call | tf_op jit(solution)/shard_map/jit(cholesky)/cholesky | solution.py:65
  188.6 9.8 %custom-call.15 = f32[1,128,128]{1,2,0:T(8,128)S(1)} custom-call(f32[1,128,128]{2,1,0:T(8,128)S(1)} %get-tuple-element.59), custom_call_target="InvertDiagBlocksLowerTriangular" | custom-call | tf_op jit(solution)/shard_map/jit(cholesky)/cholesky | solution.py:65
  203.5 3.6 all-to-all-start.1
  207.8 11.7 %cholesky.147 = f32[128,128]{1,0:T(8,128)S(1)} custom-call(f32[128,128]{1,0:T(8,128)S(1)} %convolution_subtract_fusion.5), custom_call_target="Cholesky" | custom-call | tf_op jit(solution)/shard_map/jit(cholesky)/cholesky | solution.py:65
  224.3 4.0 while.4
  228.3 19.7 %custom-call.16 = f32[2,128,128]{1,2,0:T(8,128)S(1)} custom-call(f32[2,128,128]{2,1,0:T(8,128)S(1)} %get-tuple-element.20), custom_call_target="InvertDiagBlocksLowerTriangular" | custom-call | tf_op jit(solution)/shard_map/jit(_cho_solve)/triangular_solve | solution.py:66
  249.6 12.0 %reduce-scatter.3.cloned.1.call-done = f32[512,64]{0,1:T(8,128)} async-done(((f32[4096,64]{0,1:T(8,128)}), f32[512,64]{0,1:T(8,128)}) %reduce-scatter.3.cloned.1.call-update) | async-done | bytes 131088 | tf_op jit(solution)/shard_map/reduce_scatter | solution.py:51
  263.2 4.6 all-to-all-start.2
  268.1 5.7 %all-to-all-done.2 = f32[4,128,64]{1,2,0:T(8,128)S(1)} async-done(((f32[4,128,64]{1,2,0:T(8,128)}), f32[4,128,64]{1,2,0:T(8,128)S(1)}, u32[]{:S(2)}, u32[]{:S(2)}) %all-to-all-start.2) | async-done | bytes 131104 | tf_op jit(solution)/shard_map/all_to_all | solution.py:76
  279.1 3.9 all-to-all-done.10
  287.9 122.6 %all-reduce.6.cloned.1.call-done = f32[256,256]{0,1:T(8,128)} async-done(((f32[256,256]{0,1:T(8,128)}), f32[256,256]{0,1:T(8,128)}) %all-reduce.6.cloned.1.call-update) | async-done | bytes 262160 | tf_op jit(solution)/shard_map/psum | solution.py:61
  413.6 10.0 %all_gather.7 = bf16[4096,64]{0,1:T(8,128)(2,1)S(1)} all-gather(bf16[512,64]{0,1:T(8,128)(2,1)S(1)} %get-tuple-element.40), channel_id=1, replica_groups=mesh['wide'=8,'narrow'=4] {'wide'}, dimensions={0}, use_global_device_ids=true | all-gather | bytes 589824 | tf_op jit(solution)/shard_map/all_gather | solution.py:22
  424.9 3.6 all-to-all-start.7
  428.5 11.7 %cholesky.164 = f32[128,128]{1,0:T(8,128)S(1)} custom-call(f32[128,128]{1,0:T(8,128)S(1)} %cholesky.197), custom_call_target="Cholesky" | custom-call | tf_op jit(solution)/shard_map/jit(cholesky)/cholesky | solution.py:65
  440.3 9.8 %custom-call.17 = f32[1,128,128]{1,2,0:T(8,128)S(1)} custom-call(f32[1,128,128]{2,1,0:T(8,128)S(1)} %get-tuple-element.55), custom_call_target="InvertDiagBlocksLowerTriangular" | custom-call | tf_op jit(solution)/shard_map/jit(cholesky)/cholesky | solution.py:65
  450.4 3.5 fusion.11
  455.2 5.1 all-to-all-start.8
  460.8 11.7 %cholesky.181 = f32[128,128]{1,0:T(8,128)S(1)} custom-call(f32[128,128]{1,0:T(8,128)S(1)} %convolution_subtract_fusion.4), custom_call_target="Cholesky" | custom-call | tf_op jit(solution)/shard_map/jit(cholesky)/cholesky | solution.py:65
  477.9 4.0 while.5
  481.9 19.7 %custom-call.18 = f32[2,128,128]{1,2,0:T(8,128)S(1)} custom-call(f32[2,128,128]{2,1,0:T(8,128)S(1)} %get-tuple-element.21), custom_call_target="InvertDiagBlocksLowerTriangular" | custom-call | tf_op jit(solution)/shard_map/jit(_cho_solve)/triangular_solve | solution.py:66
  503.2 11.4 %reduce-scatter.5.cloned.1.call-done = f32[512,64]{0,1:T(8,128)} async-done(((f32[4096,64]{0,1:T(8,128)}), f32[512,64]{0,1:T(8,128)}) %reduce-scatter.5.cloned.1.call-update) | async-done | bytes 131088 | tf_op jit(solution)/shard_map/reduce_scatter | solution.py:51
  516.1 4.6 all-to-all-start.9
  521.0 5.7 %all-to-all-done.9 = f32[4,128,64]{1,2,0:T(8,128)S(1)} async-done(((f32[4,128,64]{1,2,0:T(8,128)}), f32[4,128,64]{1,2,0:T(8,128)S(1)}, u32[]{:S(2)}, u32[]{:S(2)}) %all-to-all-start.9) | async-done | bytes 131104 | tf_op jit(solution)/shard_map/all_to_all | solution.py:76
  531.4 4.4 all-to-all-done.12
  540.6 4.5 all-to-all-done.11
  549.1 5.2 all-to-all-done.13
  (127 shorter events, 78.5 us)
Async XLA Ops:
  8.0 19.7 %copy-start = (f32[512,64]{0,1:T(8,128)S(1)}, f32[512,64]{0,1:T(8,128)}, u32[]{:S(2)}) copy-start(f32[512,64]{0,1:T(8,128)} %param.16) | copy-start | bytes 393220
  8.0 165.9 %copy-start.1 = (f32[8,256]{1,0:T(8,128)S(1)}, f32[8,256]{1,0:T(8,128)}, u32[]{:S(2)}) copy-start(f32[8,256]{1,0:T(8,128)} %param.18) | copy-start | bytes 24580
  9.6 23.9 %all-to-all-start.3 = ((f32[4,128,64]{1,2,0:T(8,128)}), f32[4,128,64]{1,2,0:T(8,128)S(1)}, u32[]{:S(2)}, u32[]{:S(2)}) async-start(f32[4,128,64]{1,2,0:T(8,128)} %copy_bitcast_fusion.8), calls=%async_computation.4 | async-start | bytes 262144 | tf_op jit(solution)/shard_map/all_to_all | solution.py:111
  33.5 11.5 %all-to-all-start.4 = ((f32[4,128,64]{1,2,0:T(8,128)}), f32[4,128,64]{1,2,0:T(8,128)S(1)}, u32[]{:S(2)}, u32[]{:S(2)}) async-start(f32[4,128,64]{1,2,0:T(8,128)} %copy_bitcast_fusion.7), calls=%async_computation.5 | async-start | bytes 262144 | tf_op jit(solution)/shard_map/all_to_all | solution.py:109
  38.6 135.3 %all-reduce.4.cloned.1.call-start = ((), (), s32[]{:S(2)}) async-start(), calls=%async_computation.17 | async-start | bytes 524288 | tf_op jit(solution)/shard_map/psum | solution.py:61
  45.1 9.3 %all-to-all-start.5 = ((f32[4,128,64]{1,2,0:T(8,128)}), f32[4,128,64]{1,2,0:T(8,128)S(1)}, u32[]{:S(2)}, u32[]{:S(2)}) async-start(f32[4,128,64]{1,2,0:T(8,128)} %copy_bitcast_fusion.6), calls=%async_computation.6 | async-start | bytes 262144 | tf_op jit(solution)/shard_map/all_to_all | solution.py:110
  54.3 144.3 %all-to-all-start = ((bf16[4,512,64]{1,2,0:T(8,128)(2,1)}), bf16[4,512,64]{1,2,0:T(8,128)(2,1)S(1)}, u32[]{:S(2)}, u32[]{:S(2)}) async-start(bf16[4,512,64]{1,2,0:T(8,128)(2,1)} %copy.173), calls=%async_computation | async-start | bytes 524288 | tf_op jit(solution)/shard_map/all_to_all | solution.py:31
  203.5 18.1 %all-to-all-start.1 = ((f32[1,512,256]{1,0,2:T(1,128)}), f32[1,512,256]{1,0,2:T(1,128)S(1)}, u32[]{:S(2)}, u32[]{:S(2)}) async-start(f32[1,512,256]{1,0,2:T(1,128)} %copy.174), calls=%async_computation.1 | async-start | bytes 1048576 | tf_op jit(solution)/shard_map/all_to_all | solution.py:44
  207.1 54.6 %reduce-scatter.3.cloned.1.call-start = ((), (), s32[]{:S(2)}) async-start(), calls=%async_computation.16 | async-start | bytes 1179648 | tf_op jit(solution)/shard_map/reduce_scatter | solution.py:51
  263.2 10.5 %all-to-all-start.2 = ((f32[4,128,64]{1,2,0:T(8,128)}), f32[4,128,64]{1,2,0:T(8,128)S(1)}, u32[]{:S(2)}, u32[]{:S(2)}) async-start(f32[4,128,64]{1,2,0:T(8,128)} %copy_bitcast_fusion.9), calls=%async_computation.3 | async-start | bytes 262144 | tf_op jit(solution)/shard_map/all_to_all | solution.py:76
  273.7 9.2 %all-to-all-start.10 = ((f32[4,128,64]{1,2,0:T(8,128)}), f32[4,128,64]{1,2,0:T(8,128)S(1)}, u32[]{:S(2)}, u32[]{:S(2)}) async-start(f32[4,128,64]{1,2,0:T(8,128)} %copy_bitcast_fusion.4), calls=%async_computation.12 | async-start | bytes 262144 | tf_op jit(solution)/shard_map/all_to_all | solution.py:112
  277.1 133.4 %all-reduce.6.cloned.1.call-start = ((), (), s32[]{:S(2)}) async-start(), calls=%async_computation.19 | async-start | bytes 524288 | tf_op jit(solution)/shard_map/psum | solution.py:61
  283.8 129.1 %all-to-all-start.6 = ((f32[128,4,64]{0,2,1:T(8,128)}), f32[128,4,64]{0,2,1:T(8,128)S(1)}, u32[]{:S(2)}, u32[]{:S(2)}) async-start(f32[128,4,64]{0,2,1:T(8,128)} %bitcast.28), calls=%async_computation.7 | async-start | bytes 262144 | tf_op jit(solution)/shard_map/all_to_all | solution.py:85
  424.9 25.5 %all-to-all-start.7 = ((bf16[4,512,64]{1,2,0:T(8,128)(2,1)}), bf16[4,512,64]{1,2,0:T(8,128)(2,1)S(1)}, u32[]{:S(2)}, u32[]{:S(2)}) async-start(bf16[4,512,64]{1,2,0:T(8,128)(2,1)} %copy.192), calls=%async_computation.8 | async-start | bytes 524288 | tf_op jit(solution)/shard_map/all_to_all | solution.py:31
  455.2 20.0 %all-to-all-start.8 = ((f32[1,512,256]{1,0,2:T(1,128)}), f32[1,512,256]{1,0,2:T(1,128)S(1)}, u32[]{:S(2)}, u32[]{:S(2)}) async-start(f32[1,512,256]{1,0,2:T(1,128)} %copy.193), calls=%async_computation.9 | async-start | bytes 1048576 | tf_op jit(solution)/shard_map/all_to_all | solution.py:44
  460.3 54.2 %reduce-scatter.5.cloned.1.call-start = ((), (), s32[]{:S(2)}) async-start(), calls=%async_computation.18 | async-start | bytes 1179648 | tf_op jit(solution)/shard_map/reduce_scatter | solution.py:51
  516.1 10.5 %all-to-all-start.9 = ((f32[4,128,64]{1,2,0:T(8,128)}), f32[4,128,64]{1,2,0:T(8,128)S(1)}, u32[]{:S(2)}, u32[]{:S(2)}) async-start(f32[4,128,64]{1,2,0:T(8,128)} %copy_bitcast_fusion.5), calls=%async_computation.11 | async-start | bytes 262144 | tf_op jit(solution)/shard_map/all_to_all | solution.py:76
  526.6 9.2 %all-to-all-start.12 = ((f32[128,4,64]{0,2,1:T(8,128)}), f32[128,4,64]{0,2,1:T(8,128)S(1)}, u32[]{:S(2)}, u32[]{:S(2)}) async-start(f32[128,4,64]{0,2,1:T(8,128)} %bitcast.54), calls=%async_computation.14 | async-start | bytes 262144 | tf_op jit(solution)/shard_map/all_to_all | solution.py:86
  535.9 9.2 %all-to-all-start.11 = ((f32[128,4,64]{0,2,1:T(8,128)}), f32[128,4,64]{0,2,1:T(8,128)S(1)}, u32[]{:S(2)}, u32[]{:S(2)}) async-start(f32[128,4,64]{0,2,1:T(8,128)} %bitcast.52), calls=%async_computation.13 | async-start | bytes 262144 | tf_op jit(solution)/shard_map/all_to_all | solution.py:85
  545.1 9.2 %all-to-all-start.13 = ((f32[128,4,64]{0,2,1:T(8,128)}), f32[128,4,64]{0,2,1:T(8,128)S(1)}, u32[]{:S(2)}, u32[]{:S(2)}) async-start(f32[128,4,64]{0,2,1:T(8,128)} %bitcast.56), calls=%async_computation.15 | async-start | bytes 262144 | tf_op jit(solution)/shard_map/all_to_all | solution.py:86
Sparse Core Ops, SparseCore 0:
  44.9 128.9 all-reduce.3
  283.4 127.0 all-reduce.5
Sparse Core Ops, SparseCore 1:
  224.3 37.3 reduce-scatter.2
  477.9 36.6 reduce-scatter.4
where the time goes:
time: 572 us; the launch traced here: 563 us
  waiting for transfers between devices  302 us (53%)
  other arithmetic  113 us (20%)
  starting transfers between devices  57 us (10%)
  local copies, waits for them, and re-layouts  30.9 us (5%)
  between operations  20.2 us (4%)
  blocking collectives  19.8 us (3%)
  matrix products  19.7 us (3%)
    psum x2, waiting for transfers between devices, joint_gram(): total = lax.psum(local_gram, ('wide', 'narrow'))  239 us
    another operation x13, other arithmetic, joint_gram(): lower = jnp.linalg.cholesky(gram + penalty * identity)  68.5 us
    another operation x5, other arithmetic, joint_gram(): inverse = jax.scipy.linalg.cho_solve((lower, True), identity)  39.4 us
    reduce_scatter x2, waiting for transfers between devices, owner_sums(): lax.psum_scatter(placed.reshape(owned * lax.axis_size('wide'), width), 'w...  23.4 us
    all_gather x2, blocking collectives, fetch_rows(): portion = lax.all_gather(lowered, 'wide', axis=0, tiled=True)  19.8 us
  transfers between devices with their start and end apart: 18, of which 12 were waited for; matrix products, arithmetic and copies ran while one was open for 25% of the time, Pallas kernels for 0%

commit v1 on v0

--- a/solution.py
+++ b/solution.py
@@ -58,7 +58,7 @@
 
 def joint_gram(other_rows, time_factor):
     local_gram = jnp.dot(other_rows.T, other_rows, precision=lax.Precision.HIGHEST)
-    total = lax.psum(local_gram, ("wide", "narrow"))
+    total = jnp.sum(lax.all_gather(local_gram, ("wide", "narrow")), axis=0)
     gram = total * jnp.dot(time_factor.T, time_factor, precision=lax.Precision.HIGHEST)
     penalty = jnp.trace(gram) / RANK
     identity = jnp.eye(RANK, dtype=jnp.float32)

time: 572 us -> 453 us (0.79)
  waiting for transfers between devices: 302 us -> 148 us
  blocking collectives: 19.8 us -> 82 us
  starting transfers between devices: 57 us -> 34.6 us
  other arithmetic: 113 us -> 120 us
    psum x2 -> x0, waiting for transfers between devices: 239 us -> none  [joint_gram(): total = lax.psum(local_gram, ('wide', 'narrow'))]
    all_to_all x0 -> x5, blocking collectives: none -> 60.9 us  [the longest x2 26.1 us: fetch_rows(): lax.all_to_all(gathered, 'narrow', split_axis=0, concat_axis=2, tiled=True)]
    all_gather x0 -> x2, waiting for transfers between devices: none -> 58.6 us  [joint_gram(): total = jnp.sum(lax.all_gather(local_gram, ('wide', 'narrow')), axis=0)]
    reduce_scatter x2, waiting for transfers between devices: 23.4 us -> 46.7 us  [owner_sums(): lax.psum_scatter(placed.reshape(owned * lax.axis_size('wide'), width), 'w...]
    all_to_all x3 -> x0, starting transfers between devices: 13.4 us -> none  [the longest x2 7.03 us: fetch_rows(): lax.all_to_all(gathered, 'narrow', split_axis=0, concat_axis=2, tiled=True)]
    all_to_all x2 -> x1, waiting for transfers between devices: 0.01 us -> 13.1 us  [owner_sums(): lax.all_to_all(partial_value, 'narrow', split_axis=2, concat_axis=0, tile...]
    reduce_sum x0 -> x2, other arithmetic: none -> 7.86 us  [joint_gram(): total = jnp.sum(lax.all_gather(local_gram, ('wide', 'narrow')), axis=0)]
  transfers between devices with their start and end apart: 18 -> 13, of which waited for: 12 -> 10; matrix products, arithmetic and copies ran while one was open for 25% -> 18% of each run, Pallas kernels for 0% -> 0%
where the time goes in v1:
time: 453 us; the launch traced here: 446 us
  waiting for transfers between devices  148 us (33%)
  other arithmetic  120 us (26%)
  blocking collectives  82 us (18%)
  starting transfers between devices  34.6 us (8%)
  local copies, waits for them, and re-layouts  25.2 us (6%)
  between operations  20.4 us (5%)
  matrix products  16.5 us (4%)
    another operation x13, other arithmetic, joint_gram(): lower = jnp.linalg.cholesky(gram + penalty * identity)  68.6 us
    all_gather x2, waiting for transfers between devices, joint_gram(): total = jnp.sum(lax.all_gather(local_gram, ('wide', 'narrow')), axis=0)  58.6 us
    reduce_scatter x2, waiting for transfers between devices, owner_sums(): lax.psum_scatter(placed.reshape(owned * lax.axis_size('wide'), width), 'w...  46.7 us
    another operation x5, other arithmetic, joint_gram(): inverse = jax.scipy.linalg.cho_solve((lower, True), identity)  39.7 us
    all_to_all x2, blocking collectives, fetch_rows(): lax.all_to_all(gathered, 'narrow', split_axis=0, concat_axis=2, tiled=True)  26.1 us
    all_gather x2, blocking collectives, fetch_rows(): portion = lax.all_gather(lowered, 'wide', axis=0, tiled=True)  21.1 us
    all_to_all x1, blocking collectives, owner_sums(): lax.all_to_all(partial_value, 'narrow', split_axis=2, concat_axis=0, tile...  16.7 us
    all_to_all x2, waiting for transfers between devices, update_rows(): lax.all_to_all(sums, 'narrow', split_axis=0, concat_axis=1, tiled=True)  13.7 us
  transfers between devices with their start and end apart: 13, of which 10 were waited for; matrix products, arithmetic and copies ran while one was open for 18% of the time, Pallas kernels for 0%

profile of v1, /device:TPU:0, one launch (start us, length us, event | category | flops | bytes accessed | tf_op | source)
XLA Modules:
  0.0 446.4 jit_solution(10180100401966581816)
XLA Ops:
  9.0 11.3 %all_gather.18 = bf16[4096,64]{0,1:T(8,128)(2,1)S(1)} all-gather(bf16[512,64]{0,1:T(8,128)(2,1)S(1)} %convert_element_type.70), channel_id=1, replica_groups=mesh['wide'=8,'narrow'=4] {'wide'}, dimensions={0}, use_global_device_ids=true | all-gather | bytes 589824 | tf_op jit(solution)/shard_map/all_gather | solution.py:22
  22.5 14.1 %all_to_all.244 = bf16[4,512,64]{1,2,0:T(8,128)(2,1)S(1)} all-to-all(bf16[4,512,64]{1,2,0:T(8,128)(2,1)S(1)} %copy.167), channel_id=1, replica_groups=mesh['wide'=8,'narrow'=4] {'narrow'}, dimensions={0} | all-to-all | bytes 524288 | tf_op jit(solution)/shard_map/all_to_all | solution.py:31
  45.3 13.1 %all-to-all-done.1 = f32[1,512,256]{1,0,2:T(1,128)S(1)} async-done(((f32[1,512,256]{1,0,2:T(1,128)}), f32[1,512,256]{1,0,2:T(1,128)S(1)}, u32[]{:S(2)}, u32[]{:S(2)}) %all-to-all-start.1) | async-done | bytes 524320 | tf_op jit(solution)/shard_map/all_to_all | solution.py:44
  61.3 8.5 %all_to_all.245 = f32[4,128,64]{1,2,0:T(8,128)S(1)} all-to-all(f32[4,128,64]{1,2,0:T(8,128)S(1)} %copy_bitcast_fusion.8), channel_id=1, replica_groups=mesh['wide'=8,'narrow'=4] {'narrow'}, dimensions={0} | all-to-all | bytes 262144 | tf_op jit(solution)/shard_map/all_to_all | solution.py:111
  75.5 5.3 %all-to-all-done.4 = f32[4,128,64]{1,2,0:T(8,128)S(1)} async-done(((f32[4,128,64]{1,2,0:T(8,128)}), f32[4,128,64]{1,2,0:T(8,128)S(1)}, u32[]{:S(2)}, u32[]{:S(2)}) %all-to-all-start.4) | async-done | bytes 131104 | tf_op jit(solution)/shard_map/all_to_all | solution.py:109
  84.2 11.9 %reduce-scatter.3.cloned.1.call-done = f32[512,64]{0,1:T(8,128)} async-done(((f32[4096,64]{0,1:T(8,128)}), f32[512,64]{0,1:T(8,128)}) %reduce-scatter.3.cloned.1.call-update) | async-done | bytes 131088 | tf_op jit(solution)/shard_map/reduce_scatter | solution.py:51
  97.6 4.6 %all-to-all-start.2 = ((f32[4,128,64]{1,2,0:T(8,128)}), f32[4,128,64]{1,2,0:T(8,128)S(1)}, u32[]{:S(2)}, u32[]{:S(2)}) async-start(f32[4,128,64]{1,2,0:T(8,128)} %copy_bitcast_fusion.9), calls=%async_computation.3 | async-start | bytes 262144 | tf_op jit(solution)/shard_map/all_to_all | solution.py:76
  103.0 8.8 %all-to-all-done.2 = f32[4,128,64]{1,2,0:T(8,128)S(1)} async-done(((f32[4,128,64]{1,2,0:T(8,128)}), f32[4,128,64]{1,2,0:T(8,128)S(1)}, u32[]{:S(2)}, u32[]{:S(2)}) %all-to-all-start.2) | async-done | bytes 131104 | tf_op jit(solution)/shard_map/all_to_all | solution.py:76
  111.9 35.5 %all-gather.5.cloned.1.call-done = f32[8192,256]{1,0:T(8,128)} async-done(((f32[256,256]{1,0:T(8,128)}), f32[8192,256]{1,0:T(8,128)}) %all-gather.5.cloned.1.call-update) | async-done | bytes 8388624 | tf_op jit(solution)/shard_map/all_gather | solution.py:61
  147.3 3.9 reduce_sum.54
  153.3 11.7 %cholesky.130 = f32[128,128]{1,0:T(8,128)S(1)} custom-call(f32[128,128]{1,0:T(8,128)S(1)} %cholesky.194), custom_call_target="Cholesky" | custom-call | tf_op jit(solution)/shard_map/jit(cholesky)/cholesky | solution.py:65
  165.1 9.8 %custom-call.15 = f32[1,128,128]{1,2,0:T(8,128)S(1)} custom-call(f32[1,128,128]{2,1,0:T(8,128)S(1)} %get-tuple-element.59), custom_call_target="InvertDiagBlocksLowerTriangular" | custom-call | tf_op jit(solution)/shard_map/jit(cholesky)/cholesky | solution.py:65
  175.4 11.7 %cholesky.147 = f32[128,128]{1,0:T(8,128)S(1)} custom-call(f32[128,128]{1,0:T(8,128)S(1)} %convolution_subtract_fusion.5), custom_call_target="Cholesky" | custom-call | tf_op jit(solution)/shard_map/jit(cholesky)/cholesky | solution.py:65
  189.2 4.2 while.4
  193.4 19.7 %custom-call.16 = f32[2,128,128]{1,2,0:T(8,128)S(1)} custom-call(f32[2,128,128]{2,1,0:T(8,128)S(1)} %get-tuple-element.20), custom_call_target="InvertDiagBlocksLowerTriangular" | custom-call | tf_op jit(solution)/shard_map/jit(_cho_solve)/triangular_solve | solution.py:66
  215.6 9.6 %all_to_all.246 = f32[128,4,64]{0,2,1:T(8,128)S(1)} all-to-all(f32[128,4,64]{0,2,1:T(8,128)S(1)} %bitcast.257), channel_id=1, replica_groups=mesh['wide'=8,'narrow'=4] {'narrow'}, dimensions={1} | all-to-all | bytes 262144 | tf_op jit(solution)/shard_map/all_to_all | solution.py:85
  225.9 9.8 %all_gather.21 = bf16[4096,64]{0,1:T(8,128)(2,1)S(1)} all-gather(bf16[512,64]{0,1:T(8,128)(2,1)S(1)} %get-tuple-element.40), channel_id=1, replica_groups=mesh['wide'=8,'narrow'=4] {'wide'}, dimensions={0}, use_global_device_ids=true | all-gather | bytes 589824 | tf_op jit(solution)/shard_map/all_gather | solution.py:22
  236.3 12.1 %all_to_all.247 = bf16[4,512,64]{1,2,0:T(8,128)(2,1)S(1)} all-to-all(bf16[4,512,64]{1,2,0:T(8,128)(2,1)S(1)} %copy.186), channel_id=1, replica_groups=mesh['wide'=8,'narrow'=4] {'narrow'}, dimensions={0} | all-to-all | bytes 524288 | tf_op jit(solution)/shard_map/all_to_all | solution.py:31
  250.3 16.7 %all_to_all.248 = f32[1,512,256]{1,0,2:T(1,128)S(1)} all-to-all(f32[1,512,256]{1,0,2:T(1,128)S(1)} %copy.187), channel_id=1, replica_groups=mesh['wide'=8,'narrow'=4] {'narrow'}, dimensions={2} | all-to-all | bytes 1048576 | tf_op jit(solution)/shard_map/all_to_all | solution.py:44
  274.9 34.8 %reduce-scatter.5.cloned.1.call-done = f32[512,64]{0,1:T(8,128)} async-done(((f32[4096,64]{0,1:T(8,128)}), f32[512,64]{0,1:T(8,128)}) %reduce-scatter.5.cloned.1.call-update) | async-done | bytes 131088 | tf_op jit(solution)/shard_map/reduce_scatter | solution.py:51
  311.3 4.6 %all-to-all-start.9 = ((f32[4,128,64]{1,2,0:T(8,128)}), f32[4,128,64]{1,2,0:T(8,128)S(1)}, u32[]{:S(2)}, u32[]{:S(2)}) async-start(f32[4,128,64]{1,2,0:T(8,128)} %copy_bitcast_fusion.5), calls=%async_computation.11 | async-start | bytes 262144 | tf_op jit(solution)/shard_map/all_to_all | solution.py:76
  316.9 5.0 %all-to-all-done.9 = f32[4,128,64]{1,2,0:T(8,128)S(1)} async-done(((f32[4,128,64]{1,2,0:T(8,128)}), f32[4,128,64]{1,2,0:T(8,128)S(1)}, u32[]{:S(2)}, u32[]{:S(2)}) %all-to-all-start.9) | async-done | bytes 131104 | tf_op jit(solution)/shard_map/all_to_all | solution.py:76
  321.9 4.5 %all-to-all-start.12 = ((f32[128,4,64]{0,2,1:T(8,128)}), f32[128,4,64]{0,2,1:T(8,128)S(1)}, u32[]{:S(2)}, u32[]{:S(2)}) async-start(f32[128,4,64]{0,2,1:T(8,128)} %bitcast.56), calls=%async_computation.14 | async-start | bytes 262144 | tf_op jit(solution)/shard_map/all_to_all | solution.py:86
  326.5 23.2 %all-gather.7.cloned.1.call-done = f32[8192,256]{1,0:T(8,128)} async-done(((f32[256,256]{1,0:T(8,128)}), f32[8192,256]{1,0:T(8,128)}) %all-gather.7.cloned.1.call-update) | async-done | bytes 8388624 | tf_op jit(solution)/shard_map/all_gather | solution.py:61
  349.7 3.9 reduce_sum.56
  355.2 11.7 %cholesky.164 = f32[128,128]{1,0:T(8,128)S(1)} custom-call(f32[128,128]{1,0:T(8,128)S(1)} %cholesky.197), custom_call_target="Cholesky" | custom-call | tf_op jit(solution)/shard_map/jit(cholesky)/cholesky | solution.py:65
  367.0 9.8 %custom-call.17 = f32[1,128,128]{1,2,0:T(8,128)S(1)} custom-call(f32[1,128,128]{2,1,0:T(8,128)S(1)} %get-tuple-element.55), custom_call_target="InvertDiagBlocksLowerTriangular" | custom-call | tf_op jit(solution)/shard_map/jit(cholesky)/cholesky | solution.py:65
  377.3 11.7 %cholesky.181 = f32[128,128]{1,0:T(8,128)S(1)} custom-call(f32[128,128]{1,0:T(8,128)S(1)} %convolution_subtract_fusion.4), custom_call_target="Cholesky" | custom-call | tf_op jit(solution)/shard_map/jit(cholesky)/cholesky | solution.py:65
  391.8 4.1 while.5
  395.9 19.9 %custom-call.18 = f32[2,128,128]{1,2,0:T(8,128)S(1)} custom-call(f32[2,128,128]{2,1,0:T(8,128)S(1)} %get-tuple-element.21), custom_call_target="InvertDiagBlocksLowerTriangular" | custom-call | tf_op jit(solution)/shard_map/jit(_cho_solve)/triangular_solve | solution.py:66
  423.9 5.0 %all-to-all-done.11 = f32[128,4,64]{0,2,1:T(8,128)S(1)} async-done(((f32[128,4,64]{0,2,1:T(8,128)}), f32[128,4,64]{0,2,1:T(8,128)S(1)}, u32[]{:S(2)}, u32[]{:S(2)}) %all-to-all-start.11) | async-done | bytes 131104 | tf_op jit(solution)/shard_map/all_to_all | solution.py:85
  432.9 5.2 %all-to-all-done.13 = f32[128,4,64]{0,2,1:T(8,128)S(1)} async-done(((f32[128,4,64]{0,2,1:T(8,128)}), f32[128,4,64]{0,2,1:T(8,128)S(1)}, u32[]{:S(2)}, u32[]{:S(2)}) %all-to-all-start.13) | async-done | bytes 131104 | tf_op jit(solution)/shard_map/all_to_all | solution.py:86
  (136 shorter events, 68.4 us)
Async XLA Ops:
  8.0 62.9 %copy-start = (f32[512,64]{0,1:T(8,128)S(1)}, f32[512,64]{0,1:T(8,128)}, u32[]{:S(2)}) copy-start(f32[512,64]{0,1:T(8,128)} %param.16) | copy-start | bytes 393220
  8.0 28.6 %copy-start.4 = (f32[8,256]{1,0:T(8,128)S(1)}, f32[8,256]{1,0:T(8,128)}, u32[]{:S(2)}) copy-start(f32[8,256]{1,0:T(8,128)} %param.18) | copy-start | bytes 24580
  36.6 8.5 %copy-start.6 = (s32[8]{0:T(128)S(1)}, s32[8]{0:T(128)}, u32[]{:S(2)}) copy-start(s32[8]{0:T(128)} %param.14) | copy-start | bytes 100
  40.1 21.1 %copy-start.1 = (f32[512,64]{0,1:T(8,128)S(1)}, f32[512,64]{0,1:T(8,128)}, u32[]{:S(2)}) copy-start(f32[512,64]{0,1:T(8,128)} %param.17) | copy-start | bytes 393220
  41.5 33.4 %copy-start.2 = (f32[512,64]{0,1:T(8,128)S(1)}, f32[512,64]{0,1:T(8,128)}, u32[]{:S(2)}) copy-start(f32[512,64]{0,1:T(8,128)} %param.19) | copy-start | bytes 393220
  41.5 17.0 %all-to-all-start.1 = ((f32[1,512,256]{1,0,2:T(1,128)}), f32[1,512,256]{1,0,2:T(1,128)S(1)}, u32[]{:S(2)}, u32[]{:S(2)}) async-start(f32[1,512,256]{1,0,2:T(1,128)} %copy.168), calls=%async_computation.1 | async-start | bytes 1048576 | tf_op jit(solution)/shard_map/all_to_all | solution.py:44
  45.1 51.0 %reduce-scatter.3.cloned.1.call-start = ((), (), s32[]{:S(2)}) async-start(), calls=%async_computation.16 | async-start | bytes 1179648 | tf_op jit(solution)/shard_map/reduce_scatter | solution.py:51
  61.2 86.1 %all-gather.5.cloned.1.call-start = ((), (), s32[]{:S(2)}) async-start(), calls=%async_computation.18 | async-start | bytes 8650752 | tf_op jit(solution)/shard_map/all_gather | solution.py:61
  71.5 9.3 %all-to-all-start.4 = ((f32[4,128,64]{1,2,0:T(8,128)}), f32[4,128,64]{1,2,0:T(8,128)S(1)}, u32[]{:S(2)}, u32[]{:S(2)}) async-start(f32[4,128,64]{1,2,0:T(8,128)} %copy_bitcast_fusion.7), calls=%async_computation.5 | async-start | bytes 262144 | tf_op jit(solution)/shard_map/all_to_all | solution.py:109
  80.8 16.8 %all-to-all-start.5 = ((f32[4,128,64]{1,2,0:T(8,128)}), f32[4,128,64]{1,2,0:T(8,128)S(1)}, u32[]{:S(2)}, u32[]{:S(2)}) async-start(f32[4,128,64]{1,2,0:T(8,128)} %copy_bitcast_fusion.6), calls=%async_computation.6 | async-start | bytes 262144 | tf_op jit(solution)/shard_map/all_to_all | solution.py:110
  97.6 14.1 %all-to-all-start.2 = ((f32[4,128,64]{1,2,0:T(8,128)}), f32[4,128,64]{1,2,0:T(8,128)S(1)}, u32[]{:S(2)}, u32[]{:S(2)}) async-start(f32[4,128,64]{1,2,0:T(8,128)} %copy_bitcast_fusion.9), calls=%async_computation.3 | async-start | bytes 262144 | tf_op jit(solution)/shard_map/all_to_all | solution.py:76
  102.2 207.5 %reduce-scatter.5.cloned.1.call-start = ((), (), s32[]{:S(2)}) async-start(), calls=%async_computation.17 | async-start | bytes 1179648 | tf_op jit(solution)/shard_map/reduce_scatter | solution.py:51
  215.6 32.8 %copy-start.5 = (bf16[1,8,512,512]{3,2,1,0:T(8,128)(2,1)S(1)}, bf16[1,8,512,512]{3,2,1,0:T(8,128)(2,1)}, u32[]{:S(2)}) copy-start(bf16[1,8,512,512]{3,2,1,0:T(8,128)(2,1)} %param.12) | copy-start | bytes 12582916
  249.8 21.2 %copy-start.3 = (f32[512,64]{0,1:T(8,128)S(1)}, f32[512,64]{0,1:T(8,128)}, u32[]{:S(2)}) copy-start(f32[512,64]{0,1:T(8,128)} %param.20) | copy-start | bytes 393220
  269.7 79.9 %all-gather.7.cloned.1.call-start = ((), (), s32[]{:S(2)}) async-start(), calls=%async_computation.19 | async-start | bytes 8650752 | tf_op jit(solution)/shard_map/all_gather | solution.py:61
  271.6 39.7 %all-to-all-start.10 = ((f32[4,128,64]{1,2,0:T(8,128)}), f32[4,128,64]{1,2,0:T(8,128)S(1)}, u32[]{:S(2)}, u32[]{:S(2)}) async-start(f32[4,128,64]{1,2,0:T(8,128)} %copy_bitcast_fusion.4), calls=%async_computation.12 | async-start | bytes 262144 | tf_op jit(solution)/shard_map/all_to_all | solution.py:112
  311.3 10.5 %all-to-all-start.9 = ((f32[4,128,64]{1,2,0:T(8,128)}), f32[4,128,64]{1,2,0:T(8,128)S(1)}, u32[]{:S(2)}, u32[]{:S(2)}) async-start(f32[4,128,64]{1,2,0:T(8,128)} %copy_bitcast_fusion.5), calls=%async_computation.11 | async-start | bytes 262144 | tf_op jit(solution)/shard_map/all_to_all | solution.py:76
  321.9 97.3 %all-to-all-start.12 = ((f32[128,4,64]{0,2,1:T(8,128)}), f32[128,4,64]{0,2,1:T(8,128)S(1)}, u32[]{:S(2)}, u32[]{:S(2)}) async-start(f32[128,4,64]{0,2,1:T(8,128)} %bitcast.56), calls=%async_computation.14 | async-start | bytes 262144 | tf_op jit(solution)/shard_map/all_to_all | solution.py:86
  419.1 9.7 %all-to-all-start.11 = ((f32[128,4,64]{0,2,1:T(8,128)}), f32[128,4,64]{0,2,1:T(8,128)S(1)}, u32[]{:S(2)}, u32[]{:S(2)}) async-start(f32[128,4,64]{0,2,1:T(8,128)} %bitcast.54), calls=%async_computation.13 | async-start | bytes 262144 | tf_op jit(solution)/shard_map/all_to_all | solution.py:85
  428.9 9.2 %all-to-all-start.13 = ((f32[128,4,64]{0,2,1:T(8,128)}), f32[128,4,64]{0,2,1:T(8,128)S(1)}, u32[]{:S(2)}, u32[]{:S(2)}) async-start(f32[128,4,64]{0,2,1:T(8,128)} %bitcast.58), calls=%async_computation.15 | async-start | bytes 262144 | tf_op jit(solution)/shard_map/all_to_all | solution.py:86
Sparse Core Ops, SparseCore 0:
  61.3 34.6 reduce-scatter.2
  269.9 39.8 reduce-scatter.4
Sparse Core Ops, SparseCore 1:
  70.9 76.3 all-gather.4
  273.2 76.4 all-gather.6
